TPU v7x, 256 devices: a whole 4x4x8 slice. The times are simulated.
256 devices in a mesh: gx: 32 (over x, z_hi, core), sec: 8 (over z_lo, y).
Axes of the slice: x: 4, y: 4, z: 8 (z_hi: 4, z_lo: 2; z = z_hi * 2 + z_lo), core: 2. Of those that a mesh axis runs over, the one named last changes fastest.
Arguments:
- state_init: float32 [16, 256, 64, 128], P(None, 'gx', 'sec'), may hold values from -6 to 6
- rock_type: int32 [256, 4096], P('gx', 'sec'), may hold values from 0 to 15
- perm_table: float32 [3, 16], replicated, may hold values from 0.2 to 1
- well_cells: int32 [256], replicated, may hold values from 0 to 1048575
- well_rate: float32 [16, 256], replicated, may hold values from -12 to 12
- basis_in: bfloat16 [256, 64, 128, 256], P(('gx', 'sec')), may hold values from -4 to 4
- singular: float32 [256], replicated, may hold values from 0.5 to 2
Outputs:
- state_out: float32 [16, 256, 64, 128], P(None, 'gx', 'sec')
- basis_out: bfloat16 [256, 64, 128, 256], P(('gx', 'sec'))
- singular_out: float32 [256], replicated
All inputs are finite; a program needn't handle non-finite values.
Results may differ from a plain program's by a relative error of at most 0.0059.
Values may be sent and summed in bfloat16 or wider, within the bound.
A program may use at most 128 MiB of HBM per device.

v0:
```python
import jax
import jax.numpy as jnp
from jax import lax
from jax.sharding import PartitionSpec as P

MG = 8
STEPS = 4
GROUPS = 2
DT_PRESSURE = 0.12
DT_SATURATION = 0.06
DT_ADVECT = 0.15


def with_halo(block, sides, width):
    for axis, dim in sides:
        count = lax.axis_size(axis)
        forward = [(i, i + 1) for i in range(count - 1)]
        backward = [(target, source) for source, target in forward]
        low = lax.ppermute(
            lax.slice_in_dim(block, block.shape[dim] - width, None, axis=dim), axis, forward
        )
        high = lax.ppermute(lax.slice_in_dim(block, 0, width, axis=dim), axis, backward)
        block = jnp.concatenate([low, block, high], axis=dim)
    return block


def harmonic(left, right):
    return 2.0 * left * right / (left + right)


def shift_layers(fields):
    blank = jnp.zeros_like(fields[..., :1])
    return (
        jnp.concatenate([fields[..., 1:], blank], -1),
        jnp.concatenate([blank, fields[..., :-1]], -1),
    )


def advance(fields, besides, weights, inflow, layers):
    column = lax.broadcasted_iota(jnp.int32, (fields.shape[-1],), 0)
    step_sizes = jnp.where(column < layers, DT_PRESSURE, DT_SATURATION)
    is_sat = (column >= layers).astype(fields.dtype)
    press_both = jnp.concatenate([fields[..., :layers], fields[..., :layers]], -1)
    spread = jnp.zeros_like(fields)
    carried = jnp.zeros_like(fields)
    for beside, weight in zip(besides, weights):
        spread = spread + weight * (beside - fields)
        beside_press = jnp.concatenate([beside[..., :layers], beside[..., :layers]], -1)
        pushed = weight * (beside_press - press_both)
        carried = carried + jnp.maximum(pushed, 0.0) * beside + jnp.minimum(pushed, 0.0) * fields
    return fields + step_sizes * spread + DT_ADVECT * is_sat * carried + DT_PRESSURE * inflow


HIGH = lax.Precision.HIGHEST


def hdot(a, b):
    return jnp.dot(a, b, precision=HIGH)


def batch_update(coeffs, gram_of, sigma):
    rounded = coeffs.astype(jnp.bfloat16).astype(jnp.float32)
    gram = gram_of(coeffs, rounded)
    square = jnp.diag(sigma * sigma)
    total = square + hdot(coeffs.T, coeffs)
    inner = hdot(total, total) + hdot(coeffs.T, hdot(gram, coeffs))
    factor = jnp.linalg.cholesky(inner)
    eye = jnp.eye(sigma.shape[0], dtype=jnp.float32)
    back = lax.linalg.triangular_solve(factor, eye, left_side=True, lower=True).T
    top = sigma[:, None] * hdot(total, back)
    bottom = hdot(hdot(coeffs, total) + hdot(gram, coeffs), back)
    sigma_next = jnp.sqrt(jnp.sum(top * top, axis=0) + jnp.sum(bottom * bottom, axis=0))
    on_basis = hdot(square + hdot((coeffs - rounded).T, coeffs), back)
    on_snaps = hdot(coeffs, back)
    return (on_basis, on_snaps, sigma_next)


def small_algebra(uu, su, ss, sigma):
    half = su.shape[0] // 2
    s00, s10, s11 = (ss[:half, :half], ss[half:, :half], ss[half:, half:])

    def gram_first(c, r):
        cr = hdot(c, r.T)
        return s00 - cr - cr.T + hdot(r, hdot(uu, r.T))

    wu, ws, sigma1 = batch_update(su[:half], gram_first, sigma)
    coeffs1 = hdot(su[half:], wu) + hdot(s10, ws)

    def gram_second(c, r):
        cr = hdot(c, r.T)
        yu, ys = (hdot(wu, r.T), hdot(ws, r.T))
        mixed = hdot(ys.T, hdot(su[:half], yu))
        own = hdot(yu.T, hdot(uu, yu)) + mixed + mixed.T + hdot(ys.T, hdot(s00, ys))
        return s11 - cr - cr.T + own

    wu1, ws1, sigma2 = batch_update(coeffs1, gram_second, sigma1)
    return (hdot(wu, wu1), hdot(ws, wu1), ws1, sigma2)


def body(state_init, rock_type, perm_table, well_cells, well_rate, basis_in, singular):
    across = state_init.shape[1]
    along = state_init.shape[2]
    layers = state_init.shape[3] // 2
    sec_count = lax.axis_size("sec")
    rock_count = perm_table.shape[1]
    kinds = lax.broadcasted_iota(jnp.int32, (rock_count, 1, 1), 0)
    picks = (rock_type[None] == kinds).astype(jnp.float32)
    perm = jnp.einsum("dr,rxc->dxc", perm_table, picks, precision=lax.Precision.HIGHEST).reshape(
        3, across, along, layers
    )
    paired = jnp.concatenate([perm[0], perm[1]], -1)
    bordered_perm = with_halo(paired.astype(jnp.bfloat16), (("gx", 0), ("sec", 1)), 1).astype(
        paired.dtype
    )
    perm_xh = bordered_perm[..., :layers]
    perm_yh = bordered_perm[..., layers:]
    x_up = harmonic(perm[0], perm_xh[2:, 1:-1])
    x_down = harmonic(perm_xh[:-2, 1:-1], perm[0])
    y_up = harmonic(perm[1], perm_yh[1:-1, 2:])
    y_down = harmonic(perm_yh[1:-1, :-2], perm[1])
    z_padded = jnp.pad(perm[2], ((0, 0), (0, 0), (1, 1)))
    z_up = harmonic(perm[2], z_padded[..., 2:])
    z_down = harmonic(z_padded[..., :-2], perm[2])
    weights = [
        jnp.concatenate([face, face], -1) for face in (x_up, x_down, y_up, y_down, z_up, z_down)
    ]
    x_start = lax.axis_index("gx") * across
    y_start = lax.axis_index("sec") * along
    total_y = along * sec_count
    x_pos = lax.broadcasted_iota(jnp.int32, (across, along, layers), 0)
    y_pos = lax.broadcasted_iota(jnp.int32, (across, along, layers), 1)
    z_pos = lax.broadcasted_iota(jnp.int32, (across, along, layers), 2)
    cell_ids = ((x_start + x_pos) * total_y + y_start + y_pos) * layers + z_pos
    hits = (well_cells[:, None] == cell_ids.reshape(1, -1)).astype(jnp.float32)
    source = jnp.dot(well_rate, hits, precision=lax.Precision.HIGHEST).reshape(
        state_init.shape[0], across, along, layers
    )
    source_full = jnp.concatenate([source, jnp.zeros_like(source)], -1)
    local_rows = basis_in.shape[0] * basis_in.shape[1] * basis_in.shape[2]
    rows_total = local_rows * lax.axis_size("gx") * sec_count
    finals = []
    snaps = []
    for group in range(GROUPS):
        fields = state_init[group * MG : (group + 1) * MG]
        inflow = source_full[group * MG : (group + 1) * MG]
        saved = []
        for step_index in range(STEPS):
            bordered = with_halo(fields.astype(jnp.bfloat16), (("gx", 1), ("sec", 2)), 1).astype(
                fields.dtype
            )
            up_layer, down_layer = shift_layers(fields)
            besides = [
                bordered[:, 2:, 1:-1],
                bordered[:, :-2, 1:-1],
                bordered[:, 1:-1, 2:],
                bordered[:, 1:-1, :-2],
                up_layer,
                down_layer,
            ]
            fields = advance(fields, besides, weights, inflow, layers)
            snapshot = fields.astype(jnp.bfloat16)
            saved.append(snapshot)
        finals.append(fields)
        stacked = jnp.concatenate(saved, 0)
        stacked = lax.all_to_all(stacked, "sec", split_axis=1, concat_axis=2, tiled=True)
        snaps.append(stacked.reshape(stacked.shape[0], -1))
    both = jnp.concatenate(snaps, 0)
    basis = basis_in.reshape(both.shape[1], basis_in.shape[-1])
    count = basis.shape[1]
    uu = lax.dot_general(basis, basis, (((0,), (0,)), ((), ())), preferred_element_type=jnp.float32)
    su = jnp.dot(both, basis, preferred_element_type=jnp.float32)
    ss = lax.dot_general(both, both, (((1,), (1,)), ((), ())), preferred_element_type=jnp.float32)
    local = jnp.concatenate(
        [
            jnp.concatenate([uu, su], 0),
            jnp.pad(
                jnp.concatenate([jnp.zeros((count, both.shape[0]), jnp.float32), ss], 0),
                ((0, 0), (0, 64)),
            ),
        ],
        1,
    )
    whole = lax.psum(local, ("gx", "sec")) / rows_total
    w0, w1, w2, sigma = small_algebra(
        whole[:count, :count],
        whole[count:, :count],
        whole[count:, count : count + both.shape[0]],
        singular,
    )
    fresh = jnp.dot(basis, w0.astype(jnp.bfloat16), preferred_element_type=jnp.float32)
    fresh = fresh + lax.dot_general(
        both,
        jnp.concatenate([w1, w2], 0).astype(jnp.bfloat16),
        (((0,), (0,)), ((), ())),
        preferred_element_type=jnp.float32,
    )
    basis_now = fresh.astype(jnp.bfloat16).reshape(basis_in.shape)
    return (jnp.concatenate(finals, 0), basis_now, sigma)


def solution(mesh):
    return jax.shard_map(
        body,
        mesh=mesh,
        in_specs=(
            P(None, "gx", "sec", None),
            P("gx", "sec"),
            P(),
            P(),
            P(),
            P(("gx", "sec"), None, None, None),
            P(),
        ),
        out_specs=(P(None, "gx", "sec", None), P(("gx", "sec"), None, None, None), P()),
        check_vma=False,
    )
```

profile of v0, /device:TPU:6, one launch (start us, length us, event | category | flops | bytes accessed | tf_op | source)
XLA Modules:
  0.0 627.0 jit_solution(13930910843129405325)
XLA Ops:
  11.1 7.9 %collective-permute-start.1 = (bf16[1,8,128]{2,1,0:T(8,128)(2,1)}, bf16[1,8,128]{2,1,0:T(8,128)(2,1)}, u32[]{:S(2)}, u32[]{:S(2)}) collective-permute-start(bf16[1,8,128]{2,1,0:T(8,128)(2,1)} %get-tuple-element.186), channel_id=1, source_target_pairs={{8,0},{16,8},{24,16},{32,24},{40,32},{48,40},{56,48},{64,56},{72,6... | collective-permute-start | bytes 6152 | tf_op jit(solution)/shard_map/ppermute | solution.py:22
  22.6 6.7 %collective-permute-start.5 = (bf16[8,1,8,128]{3,2,0,1:T(8,128)(2,1)}, bf16[8,1,8,128]{3,2,0,1:T(8,128)(2,1)}, u32[]{:S(2)}, u32[]{:S(2)}) collective-permute-start(bf16[8,1,8,128]{3,2,0,1:T(8,128)(2,1)} %get-tuple-element.160), channel_id=1, source_target_pairs={{8,0},{16,8},{24,16},{32,24},{40,32},{48,40},{56,48},{64,56},{72,6... | collective-permute-start | bytes 49160 | tf_op jit(solution)/shard_map/ppermute | solution.py:22
  34.6 5.5 fusion.8
  51.2 6.4 %collective-permute-start.21 = (bf16[8,1,8,128]{3,2,0,1:T(8,128)(2,1)}, bf16[8,1,8,128]{3,2,0,1:T(8,128)(2,1)S(1)}, u32[]{:S(2)}, u32[]{:S(2)}) collective-permute-start(bf16[8,1,8,128]{3,2,0,1:T(8,128)(2,1)} %get-tuple-element.168), channel_id=1, source_target_pairs={{8,0},{16,8},{24,16},{32,24},{40,32},{48,40},{56,48},{64,56},{72,6... | collective-permute-start | bytes 49160 | tf_op jit(solution)/shard_map/ppermute | solution.py:22
  59.5 4.3 collective-permute-start.6
  65.2 4.5 collective-permute-start.22
  79.1 6.7 %collective-permute-start.9 = (bf16[8,1,8,128]{3,2,0,1:T(8,128)(2,1)S(1)}, bf16[8,1,8,128]{3,2,0,1:T(8,128)(2,1)S(1)}, u32[]{:S(2)}, u32[]{:S(2)}) collective-permute-start(bf16[8,1,8,128]{3,2,0,1:T(8,128)(2,1)S(1)} %get-tuple-element.158), channel_id=1, source_target_pairs={{8,0},{16,8},{24,16},{32,24},{40,32},{48,40},{56,48},{64,56},{72,6... | collective-permute-start | bytes 49160 | tf_op jit(solution)/shard_map/ppermute | solution.py:22
  87.9 6.7 %collective-permute-start.25 = (bf16[8,1,8,128]{3,2,0,1:T(8,128)(2,1)S(1)}, bf16[8,1,8,128]{3,2,0,1:T(8,128)(2,1)S(1)}, u32[]{:S(2)}, u32[]{:S(2)}) collective-permute-start(bf16[8,1,8,128]{3,2,0,1:T(8,128)(2,1)S(1)} %get-tuple-element.166), channel_id=1, source_target_pairs={{8,0},{16,8},{24,16},{32,24},{40,32},{48,40},{56,48},{64,56},{72,6... | collective-permute-start | bytes 49160 | tf_op jit(solution)/shard_map/ppermute | solution.py:22
  99.7 6.7 %collective-permute-start.26 = (bf16[8,10,1,128]{3,2,0,1:T(2,128)(2,1)S(1)}, bf16[8,10,1,128]{3,2,0,1:T(2,128)(2,1)S(1)}, u32[]{:S(2)}, u32[]{:S(2)}) collective-permute-start(bf16[8,10,1,128]{3,2,0,1:T(2,128)(2,1)S(1)} %get-tuple-element.149), channel_id=1, source_target_pairs={{0,1},{1,2},{2,3},{3,4},{4,5},{5,6},{6,7},{8,9},{9,10},{10,11},{11... | collective-permute-start | bytes 61448 | tf_op jit(solution)/shard_map/ppermute | solution.py:19
  109.5 4.9 collective-permute-done.27
  117.9 6.7 %collective-permute-start.13 = (bf16[8,1,8,128]{3,2,0,1:T(8,128)(2,1)S(1)}, bf16[8,1,8,128]{3,2,0,1:T(8,128)(2,1)S(1)}, u32[]{:S(2)}, u32[]{:S(2)}) collective-permute-start(bf16[8,1,8,128]{3,2,0,1:T(8,128)(2,1)S(1)} %get-tuple-element.156), channel_id=1, source_target_pairs={{8,0},{16,8},{24,16},{32,24},{40,32},{48,40},{56,48},{64,56},{72,6... | collective-permute-start | bytes 49160 | tf_op jit(solution)/shard_map/ppermute | solution.py:22
  126.6 6.7 %collective-permute-start.29 = (bf16[8,1,8,128]{3,2,0,1:T(8,128)(2,1)S(1)}, bf16[8,1,8,128]{3,2,0,1:T(8,128)(2,1)S(1)}, u32[]{:S(2)}, u32[]{:S(2)}) collective-permute-start(bf16[8,1,8,128]{3,2,0,1:T(8,128)(2,1)S(1)} %get-tuple-element.164), channel_id=1, source_target_pairs={{8,0},{16,8},{24,16},{32,24},{40,32},{48,40},{56,48},{64,56},{72,6... | collective-permute-start | bytes 49160 | tf_op jit(solution)/shard_map/ppermute | solution.py:22
  138.8 6.0 collective-permute-start.30
  147.8 5.1 collective-permute-done.31
  156.4 6.7 %collective-permute-start.17 = (bf16[8,1,8,128]{3,2,0,1:T(8,128)(2,1)S(1)}, bf16[8,1,8,128]{3,2,0,1:T(8,128)(2,1)S(1)}, u32[]{:S(2)}, u32[]{:S(2)}) collective-permute-start(bf16[8,1,8,128]{3,2,0,1:T(8,128)(2,1)S(1)} %get-tuple-element.154), channel_id=1, source_target_pairs={{8,0},{16,8},{24,16},{32,24},{40,32},{48,40},{56,48},{64,56},{72,6... | collective-permute-start | bytes 49160 | tf_op jit(solution)/shard_map/ppermute | solution.py:22
  165.2 6.7 %collective-permute-start.33 = (bf16[8,1,8,128]{3,2,0,1:T(8,128)(2,1)S(1)}, bf16[8,1,8,128]{3,2,0,1:T(8,128)(2,1)S(1)}, u32[]{:S(2)}, u32[]{:S(2)}) collective-permute-start(bf16[8,1,8,128]{3,2,0,1:T(8,128)(2,1)S(1)} %get-tuple-element.162), channel_id=1, source_target_pairs={{8,0},{16,8},{24,16},{32,24},{40,32},{48,40},{56,48},{64,56},{72,6... | collective-permute-start | bytes 49160 | tf_op jit(solution)/shard_map/ppermute | solution.py:22
  177.2 4.7 collective-permute-start.34
  185.4 10.4 %all-to-all-start = ((bf16[32,8,8,128]{3,2,0,1:T(8,128)(2,1)}), bf16[32,8,8,128]{3,2,0,1:T(8,128)(2,1)S(1)}, u32[]{:S(2)}, u32[]{:S(2)}) async-start(bf16[32,8,8,128]{3,2,0,1:T(8,128)(2,1)} %pad_maximum_fusion.1), calls=%async_computation | async-start | bytes 1048576 | tf_op jit(solution)/shard_map/all_to_all | solution.py:165
  198.2 5.9 all-to-all-done
  208.5 7.3 %all-to-all-done.1 = bf16[32,8,8,128]{3,2,0,1:T(8,128)(2,1)S(1)} async-done(((bf16[32,8,8,128]{3,2,0,1:T(8,128)(2,1)}), bf16[32,8,8,128]{3,2,0,1:T(8,128)(2,1)S(1)}, u32[]{:S(2)}, u32[]{:S(2)}) %all-to-all-start.1) | async-done | bytes 524320 | tf_op jit(solution)/shard_map/all_to_all | solution.py:165
  220.6 249.7 %all-reduce.23.cloned.1.call-done = f32[320,384]{1,0:T(8,128)} async-done(((f32[320,384]{1,0:T(8,128)}), f32[320,384]{1,0:T(8,128)}) %all-reduce.23.cloned.1.call-update) | async-done | bytes 491536 | tf_op jit(solution)/shard_map/psum | solution.py:183
  474.5 11.7 %cholesky.130 = f32[128,128]{1,0:T(8,128)S(1)} custom-call(f32[128,128]{1,0:T(8,128)S(1)} %cholesky.194), custom_call_target="Cholesky" | custom-call | tf_op jit(solution)/shard_map/jit(cholesky)/cholesky | solution.py:67
  486.9 9.8 %custom-call.13 = f32[1,128,128]{1,2,0:T(8,128)S(1)} custom-call(f32[1,128,128]{2,1,0:T(8,128)S(1)} %get-tuple-element.182), custom_call_target="InvertDiagBlocksLowerTriangular" | custom-call | tf_op jit(solution)/shard_map/jit(cholesky)/cholesky | solution.py:67
  497.2 11.9 %cholesky.147 = f32[128,128]{1,0:T(8,128)S(1)} custom-call(f32[128,128]{1,0:T(8,128)S(1)} %convolution_subtract_fusion.3), custom_call_target="Cholesky" | custom-call | tf_op jit(solution)/shard_map/jit(cholesky)/cholesky | solution.py:67
  511.3 4.1 while.4
  515.4 19.7 %custom-call.14 = f32[2,128,128]{1,2,0:T(8,128)S(1)} custom-call(f32[2,128,128]{2,1,0:T(8,128)S(1)} %get-tuple-element.19), custom_call_target="InvertDiagBlocksLowerTriangular" | custom-call | tf_op jit(solution)/shard_map/triangular_solve/custom-call.0 | solution.py:69
  542.5 11.7 %cholesky.164 = f32[128,128]{1,0:T(8,128)S(1)} custom-call(f32[128,128]{1,0:T(8,128)S(1)} %cholesky.197), custom_call_target="Cholesky" | custom-call | tf_op jit(solution)/shard_map/jit(cholesky)/cholesky | solution.py:67
  554.9 9.8 %custom-call.15 = f32[1,128,128]{1,2,0:T(8,128)S(1)} custom-call(f32[1,128,128]{2,1,0:T(8,128)S(1)} %get-tuple-element.178), custom_call_target="InvertDiagBlocksLowerTriangular" | custom-call | tf_op jit(solution)/shard_map/jit(cholesky)/cholesky | solution.py:67
  565.2 11.9 %cholesky.181 = f32[128,128]{1,0:T(8,128)S(1)} custom-call(f32[128,128]{1,0:T(8,128)S(1)} %convolution_subtract_fusion.2), custom_call_target="Cholesky" | custom-call | tf_op jit(solution)/shard_map/jit(cholesky)/cholesky | solution.py:67
  579.2 4.1 while.5
  583.4 19.7 %custom-call.16 = f32[2,128,128]{1,2,0:T(8,128)S(1)} custom-call(f32[2,128,128]{2,1,0:T(8,128)S(1)} %get-tuple-element.20), custom_call_target="InvertDiagBlocksLowerTriangular" | custom-call | tf_op jit(solution)/shard_map/triangular_solve/custom-call.0 | solution.py:69
  613.0 6.4 %copy.82 = bf16[8192,256]{1,0:T(8,128)(2,1)} copy(bf16[8192,256]{0,1:T(8,128)(2,1)} %fusion) | data formatting | bytes 8388608
  (274 shorter events, 120.0 us)
Async XLA Ops:
  9.1 34.6 %collective-permute-start = (bf16[1,8,128]{2,1,0:T(8,128)(2,1)}, bf16[1,8,128]{2,1,0:T(8,128)(2,1)}, u32[]{:S(2)}, u32[]{:S(2)}) collective-permute-start(bf16[1,8,128]{2,1,0:T(8,128)(2,1)} %get-tuple-element.185), channel_id=1, source_target_pairs={{0,8},{8,16},{16,24},{24,32},{32,40},{40,48},{48,56},{56,64},{64,7... | collective-permute-start | bytes 6152 | tf_op jit(solution)/shard_map/ppermute | solution.py:19
  11.1 32.7 %collective-permute-start.1 = (bf16[1,8,128]{2,1,0:T(8,128)(2,1)}, bf16[1,8,128]{2,1,0:T(8,128)(2,1)}, u32[]{:S(2)}, u32[]{:S(2)}) collective-permute-start(bf16[1,8,128]{2,1,0:T(8,128)(2,1)} %get-tuple-element.186), channel_id=1, source_target_pairs={{8,0},{16,8},{24,16},{32,24},{40,32},{48,40},{56,48},{64,56},{72,6... | collective-permute-start | bytes 6152 | tf_op jit(solution)/shard_map/ppermute | solution.py:22
  20.7 38.0 %collective-permute-start.4 = (bf16[8,1,8,128]{3,2,0,1:T(8,128)(2,1)}, bf16[8,1,8,128]{3,2,0,1:T(8,128)(2,1)S(1)}, u32[]{:S(2)}, u32[]{:S(2)}) collective-permute-start(bf16[8,1,8,128]{3,2,0,1:T(8,128)(2,1)} %get-tuple-element.159), channel_id=1, source_target_pairs={{0,8},{8,16},{16,24},{24,32},{32,40},{40,48},{48,56},{56,64},{64,7... | collective-permute-start | bytes 49160 | tf_op jit(solution)/shard_map/ppermute | solution.py:19
  22.6 36.1 %collective-permute-start.5 = (bf16[8,1,8,128]{3,2,0,1:T(8,128)(2,1)}, bf16[8,1,8,128]{3,2,0,1:T(8,128)(2,1)}, u32[]{:S(2)}, u32[]{:S(2)}) collective-permute-start(bf16[8,1,8,128]{3,2,0,1:T(8,128)(2,1)} %get-tuple-element.160), channel_id=1, source_target_pairs={{8,0},{16,8},{24,16},{32,24},{40,32},{48,40},{56,48},{64,56},{72,6... | collective-permute-start | bytes 49160 | tf_op jit(solution)/shard_map/ppermute | solution.py:22
  29.9 35.2 %collective-permute-start.20 = (bf16[8,1,8,128]{3,2,0,1:T(8,128)(2,1)}, bf16[8,1,8,128]{3,2,0,1:T(8,128)(2,1)S(1)}, u32[]{:S(2)}, u32[]{:S(2)}) collective-permute-start(bf16[8,1,8,128]{3,2,0,1:T(8,128)(2,1)} %get-tuple-element.167), channel_id=1, source_target_pairs={{0,8},{8,16},{16,24},{24,32},{32,40},{40,48},{48,56},{56,64},{64,7... | collective-permute-start | bytes 49160 | tf_op jit(solution)/shard_map/ppermute | solution.py:19
  48.1 9.4 %collective-permute-start.3 = (bf16[10,1,128]{2,1,0:T(2,128)(2,1)S(1)}, bf16[10,1,128]{2,1,0:T(2,128)(2,1)S(1)}, u32[]{:S(2)}, u32[]{:S(2)}) collective-permute-start(bf16[10,1,128]{2,1,0:T(2,128)(2,1)S(1)} %get-tuple-element.184), channel_id=1, source_target_pairs={{1,0},{2,1},{3,2},{4,3},{5,4},{6,5},{7,6},{9,8},{10,9},{11,10},{12... | collective-permute-start | bytes 7688 | tf_op jit(solution)/shard_map/ppermute | solution.py:22
  51.2 13.9 %collective-permute-start.21 = (bf16[8,1,8,128]{3,2,0,1:T(8,128)(2,1)}, bf16[8,1,8,128]{3,2,0,1:T(8,128)(2,1)S(1)}, u32[]{:S(2)}, u32[]{:S(2)}) collective-permute-start(bf16[8,1,8,128]{3,2,0,1:T(8,128)(2,1)} %get-tuple-element.168), channel_id=1, source_target_pairs={{8,0},{16,8},{24,16},{32,24},{40,32},{48,40},{56,48},{64,56},{72,6... | collective-permute-start | bytes 49160 | tf_op jit(solution)/shard_map/ppermute | solution.py:22
  59.5 11.5 %collective-permute-start.6 = (bf16[8,10,1,128]{3,2,0,1:T(2,128)(2,1)S(1)}, bf16[8,10,1,128]{3,2,0,1:T(2,128)(2,1)S(1)}, u32[]{:S(2)}, u32[]{:S(2)}) collective-permute-start(bf16[8,10,1,128]{3,2,0,1:T(2,128)(2,1)S(1)} %get-tuple-element.143), channel_id=1, source_target_pairs={{0,1},{1,2},{2,3},{3,4},{4,5},{5,6},{6,7},{8,9},{9,10},{10,11},{11... | collective-permute-start | bytes 61448 | tf_op jit(solution)/shard_map/ppermute | solution.py:19
  65.2 9.2 %collective-permute-start.22 = (bf16[8,10,1,128]{3,2,0,1:T(2,128)(2,1)S(1)}, bf16[8,10,1,128]{3,2,0,1:T(2,128)(2,1)S(1)}, u32[]{:S(2)}, u32[]{:S(2)}) collective-permute-start(bf16[8,10,1,128]{3,2,0,1:T(2,128)(2,1)S(1)} %get-tuple-element.151), channel_id=1, source_target_pairs={{0,1},{1,2},{2,3},{3,4},{4,5},{5,6},{6,7},{8,9},{9,10},{10,11},{11... | collective-permute-start | bytes 61448 | tf_op jit(solution)/shard_map/ppermute | solution.py:19
  77.2 17.5 %collective-permute-start.8 = (bf16[8,1,8,128]{3,2,0,1:T(8,128)(2,1)S(1)}, bf16[8,1,8,128]{3,2,0,1:T(8,128)(2,1)S(1)}, u32[]{:S(2)}, u32[]{:S(2)}) collective-permute-start(bf16[8,1,8,128]{3,2,0,1:T(8,128)(2,1)S(1)} %get-tuple-element.157), channel_id=1, source_target_pairs={{0,8},{8,16},{16,24},{24,32},{32,40},{40,48},{48,56},{56,64},{64,7... | collective-permute-start | bytes 49160 | tf_op jit(solution)/shard_map/ppermute | solution.py:19
  79.1 15.5 %collective-permute-start.9 = (bf16[8,1,8,128]{3,2,0,1:T(8,128)(2,1)S(1)}, bf16[8,1,8,128]{3,2,0,1:T(8,128)(2,1)S(1)}, u32[]{:S(2)}, u32[]{:S(2)}) collective-permute-start(bf16[8,1,8,128]{3,2,0,1:T(8,128)(2,1)S(1)} %get-tuple-element.158), channel_id=1, source_target_pairs={{8,0},{16,8},{24,16},{32,24},{40,32},{48,40},{56,48},{64,56},{72,6... | collective-permute-start | bytes 49160 | tf_op jit(solution)/shard_map/ppermute | solution.py:22
  85.9 13.6 %collective-permute-start.24 = (bf16[8,1,8,128]{3,2,0,1:T(8,128)(2,1)S(1)}, bf16[8,1,8,128]{3,2,0,1:T(8,128)(2,1)S(1)}, u32[]{:S(2)}, u32[]{:S(2)}) collective-permute-start(bf16[8,1,8,128]{3,2,0,1:T(8,128)(2,1)S(1)} %get-tuple-element.165), channel_id=1, source_target_pairs={{0,8},{8,16},{16,24},{24,32},{32,40},{40,48},{48,56},{56,64},{64,7... | collective-permute-start | bytes 49160 | tf_op jit(solution)/shard_map/ppermute | solution.py:19
  87.9 11.7 %collective-permute-start.25 = (bf16[8,1,8,128]{3,2,0,1:T(8,128)(2,1)S(1)}, bf16[8,1,8,128]{3,2,0,1:T(8,128)(2,1)S(1)}, u32[]{:S(2)}, u32[]{:S(2)}) collective-permute-start(bf16[8,1,8,128]{3,2,0,1:T(8,128)(2,1)S(1)} %get-tuple-element.166), channel_id=1, source_target_pairs={{8,0},{16,8},{24,16},{32,24},{40,32},{48,40},{56,48},{64,56},{72,6... | collective-permute-start | bytes 49160 | tf_op jit(solution)/shard_map/ppermute | solution.py:22
  94.7 13.1 %collective-permute-start.10 = (bf16[8,10,1,128]{3,2,0,1:T(2,128)(2,1)S(1)}, bf16[8,10,1,128]{3,2,0,1:T(2,128)(2,1)S(1)}, u32[]{:S(2)}, u32[]{:S(2)}) collective-permute-start(bf16[8,10,1,128]{3,2,0,1:T(2,128)(2,1)S(1)} %get-tuple-element.141), channel_id=1, source_target_pairs={{0,1},{1,2},{2,3},{3,4},{4,5},{5,6},{6,7},{8,9},{9,10},{10,11},{11... | collective-permute-start | bytes 61448 | tf_op jit(solution)/shard_map/ppermute | solution.py:19
  98.3 9.5 %collective-permute-start.11 = (bf16[8,10,1,128]{3,2,0,1:T(2,128)(2,1)S(1)}, bf16[8,10,1,128]{3,2,0,1:T(2,128)(2,1)S(1)}, u32[]{:S(2)}, u32[]{:S(2)}) collective-permute-start(bf16[8,10,1,128]{3,2,0,1:T(2,128)(2,1)S(1)} %get-tuple-element.142), channel_id=1, source_target_pairs={{1,0},{2,1},{3,2},{4,3},{5,4},{6,5},{7,6},{9,8},{10,9},{11,10},{12... | collective-permute-start | bytes 61448 | tf_op jit(solution)/shard_map/ppermute | solution.py:22
  99.7 9.8 %collective-permute-start.26 = (bf16[8,10,1,128]{3,2,0,1:T(2,128)(2,1)S(1)}, bf16[8,10,1,128]{3,2,0,1:T(2,128)(2,1)S(1)}, u32[]{:S(2)}, u32[]{:S(2)}) collective-permute-start(bf16[8,10,1,128]{3,2,0,1:T(2,128)(2,1)S(1)} %get-tuple-element.149), channel_id=1, source_target_pairs={{0,1},{1,2},{2,3},{3,4},{4,5},{5,6},{6,7},{8,9},{9,10},{10,11},{11... | collective-permute-start | bytes 61448 | tf_op jit(solution)/shard_map/ppermute | solution.py:19
  116.0 17.5 %collective-permute-start.12 = (bf16[8,1,8,128]{3,2,0,1:T(8,128)(2,1)S(1)}, bf16[8,1,8,128]{3,2,0,1:T(8,128)(2,1)S(1)}, u32[]{:S(2)}, u32[]{:S(2)}) collective-permute-start(bf16[8,1,8,128]{3,2,0,1:T(8,128)(2,1)S(1)} %get-tuple-element.155), channel_id=1, source_target_pairs={{0,8},{8,16},{16,24},{24,32},{32,40},{40,48},{48,56},{56,64},{64,7... | collective-permute-start | bytes 49160 | tf_op jit(solution)/shard_map/ppermute | solution.py:19
  117.9 15.5 %collective-permute-start.13 = (bf16[8,1,8,128]{3,2,0,1:T(8,128)(2,1)S(1)}, bf16[8,1,8,128]{3,2,0,1:T(8,128)(2,1)S(1)}, u32[]{:S(2)}, u32[]{:S(2)}) collective-permute-start(bf16[8,1,8,128]{3,2,0,1:T(8,128)(2,1)S(1)} %get-tuple-element.156), channel_id=1, source_target_pairs={{8,0},{16,8},{24,16},{32,24},{40,32},{48,40},{56,48},{64,56},{72,6... | collective-permute-start | bytes 49160 | tf_op jit(solution)/shard_map/ppermute | solution.py:22
  124.7 14.0 %collective-permute-start.28 = (bf16[8,1,8,128]{3,2,0,1:T(8,128)(2,1)S(1)}, bf16[8,1,8,128]{3,2,0,1:T(8,128)(2,1)S(1)}, u32[]{:S(2)}, u32[]{:S(2)}) collective-permute-start(bf16[8,1,8,128]{3,2,0,1:T(8,128)(2,1)S(1)} %get-tuple-element.163), channel_id=1, source_target_pairs={{0,8},{8,16},{16,24},{24,32},{32,40},{40,48},{48,56},{56,64},{64,7... | collective-permute-start | bytes 49160 | tf_op jit(solution)/shard_map/ppermute | solution.py:19
  126.6 12.1 %collective-permute-start.29 = (bf16[8,1,8,128]{3,2,0,1:T(8,128)(2,1)S(1)}, bf16[8,1,8,128]{3,2,0,1:T(8,128)(2,1)S(1)}, u32[]{:S(2)}, u32[]{:S(2)}) collective-permute-start(bf16[8,1,8,128]{3,2,0,1:T(8,128)(2,1)S(1)} %get-tuple-element.164), channel_id=1, source_target_pairs={{8,0},{16,8},{24,16},{32,24},{40,32},{48,40},{56,48},{64,56},{72,6... | collective-permute-start | bytes 49160 | tf_op jit(solution)/shard_map/ppermute | solution.py:22
  133.5 12.6 %collective-permute-start.14 = (bf16[8,10,1,128]{3,2,0,1:T(2,128)(2,1)S(1)}, bf16[8,10,1,128]{3,2,0,1:T(2,128)(2,1)S(1)}, u32[]{:S(2)}, u32[]{:S(2)}) collective-permute-start(bf16[8,10,1,128]{3,2,0,1:T(2,128)(2,1)S(1)} %get-tuple-element.139), channel_id=1, source_target_pairs={{0,1},{1,2},{2,3},{3,4},{4,5},{5,6},{6,7},{8,9},{9,10},{10,11},{11... | collective-permute-start | bytes 61448 | tf_op jit(solution)/shard_map/ppermute | solution.py:19
  138.8 9.0 %collective-permute-start.30 = (bf16[8,10,1,128]{3,2,0,1:T(2,128)(2,1)S(1)}, bf16[8,10,1,128]{3,2,0,1:T(2,128)(2,1)S(1)}, u32[]{:S(2)}, u32[]{:S(2)}) collective-permute-start(bf16[8,10,1,128]{3,2,0,1:T(2,128)(2,1)S(1)} %get-tuple-element.147), channel_id=1, source_target_pairs={{0,1},{1,2},{2,3},{3,4},{4,5},{5,6},{6,7},{8,9},{9,10},{10,11},{11... | collective-permute-start | bytes 61448 | tf_op jit(solution)/shard_map/ppermute | solution.py:19
  154.5 17.3 %collective-permute-start.16 = (bf16[8,1,8,128]{3,2,0,1:T(8,128)(2,1)S(1)}, bf16[8,1,8,128]{3,2,0,1:T(8,128)(2,1)S(1)}, u32[]{:S(2)}, u32[]{:S(2)}) collective-permute-start(bf16[8,1,8,128]{3,2,0,1:T(8,128)(2,1)S(1)} %get-tuple-element.153), channel_id=1, source_target_pairs={{0,8},{8,16},{16,24},{24,32},{32,40},{40,48},{48,56},{56,64},{64,7... | collective-permute-start | bytes 49160 | tf_op jit(solution)/shard_map/ppermute | solution.py:19
  156.4 15.4 %collective-permute-start.17 = (bf16[8,1,8,128]{3,2,0,1:T(8,128)(2,1)S(1)}, bf16[8,1,8,128]{3,2,0,1:T(8,128)(2,1)S(1)}, u32[]{:S(2)}, u32[]{:S(2)}) collective-permute-start(bf16[8,1,8,128]{3,2,0,1:T(8,128)(2,1)S(1)} %get-tuple-element.154), channel_id=1, source_target_pairs={{8,0},{16,8},{24,16},{32,24},{40,32},{48,40},{56,48},{64,56},{72,6... | collective-permute-start | bytes 49160 | tf_op jit(solution)/shard_map/ppermute | solution.py:22
  163.2 13.9 %collective-permute-start.32 = (bf16[8,1,8,128]{3,2,0,1:T(8,128)(2,1)S(1)}, bf16[8,1,8,128]{3,2,0,1:T(8,128)(2,1)S(1)}, u32[]{:S(2)}, u32[]{:S(2)}) collective-permute-start(bf16[8,1,8,128]{3,2,0,1:T(8,128)(2,1)S(1)} %get-tuple-element.161), channel_id=1, source_target_pairs={{0,8},{8,16},{16,24},{24,32},{32,40},{40,48},{48,56},{56,64},{64,7... | collective-permute-start | bytes 49160 | tf_op jit(solution)/shard_map/ppermute | solution.py:19
  165.2 12.0 %collective-permute-start.33 = (bf16[8,1,8,128]{3,2,0,1:T(8,128)(2,1)S(1)}, bf16[8,1,8,128]{3,2,0,1:T(8,128)(2,1)S(1)}, u32[]{:S(2)}, u32[]{:S(2)}) collective-permute-start(bf16[8,1,8,128]{3,2,0,1:T(8,128)(2,1)S(1)} %get-tuple-element.162), channel_id=1, source_target_pairs={{8,0},{16,8},{24,16},{32,24},{40,32},{48,40},{56,48},{64,56},{72,6... | collective-permute-start | bytes 49160 | tf_op jit(solution)/shard_map/ppermute | solution.py:22
  171.9 11.3 %collective-permute-start.18 = (bf16[8,10,1,128]{3,2,0,1:T(2,128)(2,1)S(1)}, bf16[8,10,1,128]{3,2,0,1:T(2,128)(2,1)S(1)}, u32[]{:S(2)}, u32[]{:S(2)}) collective-permute-start(bf16[8,10,1,128]{3,2,0,1:T(2,128)(2,1)S(1)} %get-tuple-element.137), channel_id=1, source_target_pairs={{0,1},{1,2},{2,3},{3,4},{4,5},{5,6},{6,7},{8,9},{9,10},{10,11},{11... | collective-permute-start | bytes 61448 | tf_op jit(solution)/shard_map/ppermute | solution.py:19
  177.2 18.7 %collective-permute-start.34 = (bf16[8,10,1,128]{3,2,0,1:T(2,128)(2,1)S(1)}, bf16[8,10,1,128]{3,2,0,1:T(2,128)(2,1)S(1)}, u32[]{:S(2)}, u32[]{:S(2)}) collective-permute-start(bf16[8,10,1,128]{3,2,0,1:T(2,128)(2,1)S(1)} %get-tuple-element.145), channel_id=1, source_target_pairs={{0,1},{1,2},{2,3},{3,4},{4,5},{5,6},{6,7},{8,9},{9,10},{10,11},{11... | collective-permute-start | bytes 61448 | tf_op jit(solution)/shard_map/ppermute | solution.py:19
  181.9 14.1 %collective-permute-start.35 = (bf16[8,10,1,128]{3,2,0,1:T(2,128)(2,1)S(1)}, bf16[8,10,1,128]{3,2,0,1:T(2,128)(2,1)S(1)}, u32[]{:S(2)}, u32[]{:S(2)}) collective-permute-start(bf16[8,10,1,128]{3,2,0,1:T(2,128)(2,1)S(1)} %get-tuple-element.146), channel_id=1, source_target_pairs={{1,0},{2,1},{3,2},{4,3},{5,4},{6,5},{7,6},{9,8},{10,9},{11,10},{12... | collective-permute-start | bytes 61448 | tf_op jit(solution)/shard_map/ppermute | solution.py:22
  185.4 18.6 %all-to-all-start = ((bf16[32,8,8,128]{3,2,0,1:T(8,128)(2,1)}), bf16[32,8,8,128]{3,2,0,1:T(8,128)(2,1)S(1)}, u32[]{:S(2)}, u32[]{:S(2)}) async-start(bf16[32,8,8,128]{3,2,0,1:T(8,128)(2,1)} %pad_maximum_fusion.1), calls=%async_computation | async-start | bytes 1048576 | tf_op jit(solution)/shard_map/all_to_all | solution.py:165
  204.1 11.7 %all-to-all-start.1 = ((bf16[32,8,8,128]{3,2,0,1:T(8,128)(2,1)}), bf16[32,8,8,128]{3,2,0,1:T(8,128)(2,1)S(1)}, u32[]{:S(2)}, u32[]{:S(2)}) async-start(bf16[32,8,8,128]{3,2,0,1:T(8,128)(2,1)} %pad_maximum_fusion.2), calls=%async_computation.1 | async-start | bytes 1048576 | tf_op jit(solution)/shard_map/all_to_all | solution.py:165
  207.6 262.7 %all-reduce.23.cloned.1.call-start = ((), (), s32[]{:S(2)}) async-start(), calls=%async_computation.2 | async-start | bytes 983040 | tf_op jit(solution)/shard_map/psum | solution.py:183
  (21 other events, 270.8 us)
Sparse Core Ops, SparseCore 0:
  219.8 250.5 all-reduce.22
where the time goes:
time: 635 us; the launch traced here: 627 us
  waiting for transfers between devices  274 us (43%)
  starting transfers between devices  145 us (23%)
  other arithmetic  131 us (21%)
  matrix products  30.2 us (5%)
  local copies, waits for them, and re-layouts  27.9 us (4%)
  between operations  18.7 us (3%)
    psum x1, waiting for transfers between devices, body(): whole = lax.psum(local, ('gx', 'sec')) / rows_total  250 us
    ppermute x18, starting transfers between devices, with_halo(): lax.ppermute(lax.slice_in_dim(block, 0, width, axis=dim), axis, backward)  72.6 us
    another operation x14, other arithmetic, batch_update(): factor = jnp.linalg.cholesky(inner)  69.7 us
    ppermute x18, starting transfers between devices, with_halo(): lax.ppermute(lax.slice_in_dim(block, block.shape[dim] - width, None, axis...  58.3 us
    another operation x5, other arithmetic, batch_update(): lax.linalg.triangular_solve(factor, eye, left_side=True, lower=True)  39.4 us
    all_to_all x2, starting transfers between devices, body(): lax.all_to_all(stacked, 'sec', split_axis=1, concat_axis=2, tiled=True)  13.9 us
    all_to_all x2, waiting for transfers between devices, body(): lax.all_to_all(stacked, 'sec', split_axis=1, concat_axis=2, tiled=True)  13.2 us
  transfers between devices with their start and end apart: 39, of which 6 were waited for; matrix products, arithmetic and copies ran while one was open for 5% of the time, Pallas kernels for 0%

commit v1 on v0

--- a/solution.py
+++ b/solution.py
@@ -180,7 +180,7 @@
         ],
         1,
     )
-    whole = lax.psum(local, ("gx", "sec")) / rows_total
+    whole = lax.psum(lax.psum(local, "gx"), "sec") / rows_total
     w0, w1, w2, sigma = small_algebra(
         whole[:count, :count],
         whole[count:, :count],

time: 635 us -> 739 us (1.16)
  waiting for transfers between devices: 274 us -> 382 us
    psum x1 -> x2, waiting for transfers between devices: 250 us -> 356 us  [body(): whole = lax.psum(lax.psum(local, 'gx'), 'sec') / rows_total]
  transfers between devices with their start and end apart: 39 -> 40, of which waited for: 6 -> 7; matrix products, arithmetic and copies ran while one was open for 5% -> 4% of each run, Pallas kernels for 0% -> 0%
where the time goes in v1:
time: 739 us; the launch traced here: 729 us
  waiting for transfers between devices  382 us (52%)
  starting transfers between devices  145 us (20%)
  other arithmetic  126 us (17%)
  matrix products  30.2 us (4%)
  local copies, waits for them, and re-layouts  26.3 us (4%)
  between operations  18.6 us (3%)
    psum x2, waiting for transfers between devices, body(): whole = lax.psum(lax.psum(local, 'gx'), 'sec') / rows_total  356 us
    ppermute x18, starting transfers between devices, with_halo(): lax.ppermute(lax.slice_in_dim(block, 0, width, axis=dim), axis, backward)  72.5 us
    another operation x14, other arithmetic, batch_update(): factor = jnp.linalg.cholesky(inner)  69.6 us
    ppermute x18, starting transfers between devices, with_halo(): lax.ppermute(lax.slice_in_dim(block, block.shape[dim] - width, None, axis...  57.8 us
    another operation x5, other arithmetic, batch_update(): lax.linalg.triangular_solve(factor, eye, left_side=True, lower=True)  39.4 us
  transfers between devices with their start and end apart: 40, of which 7 were waited for; matrix products, arithmetic and copies ran while one was open for 4% of the time, Pallas kernels for 0%

profile of v1, /device:TPU:6, one launch (start us, length us, event | category | flops | bytes accessed | tf_op | source)
XLA Modules:
  0.0 728.5 jit_solution(16137149236737078778)
XLA Ops:
  10.5 7.9 %collective-permute-start.1 = (bf16[1,8,128]{2,1,0:T(8,128)(2,1)S(1)}, bf16[1,8,128]{2,1,0:T(8,128)(2,1)S(1)}, u32[]{:S(2)}, u32[]{:S(2)}) collective-permute-start(bf16[1,8,128]{2,1,0:T(8,128)(2,1)S(1)} %get-tuple-element.186), channel_id=1, source_target_pairs={{8,0},{16,8},{24,16},{32,24},{40,32},{48,40},{56,48},{64,56},{72,6... | collective-permute-start | bytes 6152 | tf_op jit(solution)/shard_map/ppermute | solution.py:22
  21.4 6.7 collective-permute-start.5
  32.8 5.5 fusion.8
  48.1 6.4 collective-permute-start.21
  54.9 4.3 collective-permute-start.6
  60.6 4.5 collective-permute-start.22
  74.5 6.7 collective-permute-start.9
  83.3 6.7 collective-permute-start.25
  95.1 6.7 collective-permute-start.26
  104.7 5.0 collective-permute-done.27
  113.5 6.7 collective-permute-start.13
  122.3 6.7 collective-permute-start.29
  134.5 5.3 collective-permute-start.30
  142.7 5.1 collective-permute-done.31
  151.4 6.7 collective-permute-start.17
  160.2 6.7 collective-permute-start.33
  172.2 4.7 collective-permute-start.34
  180.4 10.4 %all-to-all-start = ((bf16[32,8,8,128]{3,2,0,1:T(8,128)(2,1)}), bf16[32,8,8,128]{3,2,0,1:T(8,128)(2,1)S(1)}, u32[]{:S(2)}, u32[]{:S(2)}) async-start(bf16[32,8,8,128]{3,2,0,1:T(8,128)(2,1)} %pad_maximum_fusion.1), calls=%async_computation | async-start | bytes 1048576 | tf_op jit(solution)/shard_map/all_to_all | solution.py:165
  193.1 5.9 all-to-all-done
  203.0 7.7 %all-to-all-done.1 = bf16[32,8,8,128]{3,2,0,1:T(8,128)(2,1)S(1)} async-done(((bf16[32,8,8,128]{3,2,0,1:T(8,128)(2,1)}), bf16[32,8,8,128]{3,2,0,1:T(8,128)(2,1)S(1)}, u32[]{:S(2)}, u32[]{:S(2)}) %all-to-all-start.1) | async-done | bytes 524320 | tf_op jit(solution)/shard_map/all_to_all | solution.py:165
  215.1 264.8 %all-reduce.24.cloned.1.call-done = f32[320,384]{1,0:T(8,128)} async-done(((f32[320,384]{1,0:T(8,128)}), f32[320,384]{1,0:T(8,128)}) %all-reduce.24.cloned.1.call-update) | async-done | bytes 491536 | tf_op jit(solution)/shard_map/psum | solution.py:183
  480.9 91.5 %all-reduce.26.cloned.1.call-done = f32[320,384]{1,0:T(8,128)} async-done(((f32[320,384]{1,0:T(8,128)}), f32[320,384]{1,0:T(8,128)}) %all-reduce.26.cloned.1.call-update) | async-done | bytes 491536 | tf_op jit(solution)/shard_map/psum | solution.py:183
  576.6 11.7 %cholesky.130 = f32[128,128]{1,0:T(8,128)S(1)} custom-call(f32[128,128]{1,0:T(8,128)S(1)} %cholesky.194), custom_call_target="Cholesky" | custom-call | tf_op jit(solution)/shard_map/jit(cholesky)/cholesky | solution.py:67
  589.0 9.8 %custom-call.13 = f32[1,128,128]{1,2,0:T(8,128)S(1)} custom-call(f32[1,128,128]{2,1,0:T(8,128)S(1)} %get-tuple-element.182), custom_call_target="InvertDiagBlocksLowerTriangular" | custom-call | tf_op jit(solution)/shard_map/jit(cholesky)/cholesky | solution.py:67
  599.3 11.9 %cholesky.147 = f32[128,128]{1,0:T(8,128)S(1)} custom-call(f32[128,128]{1,0:T(8,128)S(1)} %convolution_subtract_fusion.3), custom_call_target="Cholesky" | custom-call | tf_op jit(solution)/shard_map/jit(cholesky)/cholesky | solution.py:67
  617.1 19.7 %custom-call.14 = f32[2,128,128]{1,2,0:T(8,128)S(1)} custom-call(f32[2,128,128]{2,1,0:T(8,128)S(1)} %get-tuple-element.19), custom_call_target="InvertDiagBlocksLowerTriangular" | custom-call | tf_op jit(solution)/shard_map/triangular_solve/custom-call.0 | solution.py:69
  644.1 11.7 %cholesky.164 = f32[128,128]{1,0:T(8,128)S(1)} custom-call(f32[128,128]{1,0:T(8,128)S(1)} %cholesky.197), custom_call_target="Cholesky" | custom-call | tf_op jit(solution)/shard_map/jit(cholesky)/cholesky | solution.py:67
  656.5 9.8 %custom-call.15 = f32[1,128,128]{1,2,0:T(8,128)S(1)} custom-call(f32[1,128,128]{2,1,0:T(8,128)S(1)} %get-tuple-element.178), custom_call_target="InvertDiagBlocksLowerTriangular" | custom-call | tf_op jit(solution)/shard_map/jit(cholesky)/cholesky | solution.py:67
  666.8 11.9 %cholesky.181 = f32[128,128]{1,0:T(8,128)S(1)} custom-call(f32[128,128]{1,0:T(8,128)S(1)} %convolution_subtract_fusion.2), custom_call_target="Cholesky" | custom-call | tf_op jit(solution)/shard_map/jit(cholesky)/cholesky | solution.py:67
  680.8 4.0 while.5
  684.8 19.7 %custom-call.16 = f32[2,128,128]{1,2,0:T(8,128)S(1)} custom-call(f32[2,128,128]{2,1,0:T(8,128)S(1)} %get-tuple-element.20), custom_call_target="InvertDiagBlocksLowerTriangular" | custom-call | tf_op jit(solution)/shard_map/triangular_solve/custom-call.0 | solution.py:69
  714.4 6.4 copy.82
  (269 shorter events, 118.9 us)
Async XLA Ops:
  8.6 33.4 %collective-permute-start = (bf16[1,8,128]{2,1,0:T(8,128)(2,1)S(1)}, bf16[1,8,128]{2,1,0:T(8,128)(2,1)S(1)}, u32[]{:S(2)}, u32[]{:S(2)}) collective-permute-start(bf16[1,8,128]{2,1,0:T(8,128)(2,1)S(1)} %get-tuple-element.185), channel_id=1, source_target_pairs={{0,8},{8,16},{16,24},{24,32},{32,40},{40,48},{48,56},{56,64},{64,7... | collective-permute-start | bytes 6152 | tf_op jit(solution)/shard_map/ppermute | solution.py:19
  10.5 31.5 %collective-permute-start.1 = (bf16[1,8,128]{2,1,0:T(8,128)(2,1)S(1)}, bf16[1,8,128]{2,1,0:T(8,128)(2,1)S(1)}, u32[]{:S(2)}, u32[]{:S(2)}) collective-permute-start(bf16[1,8,128]{2,1,0:T(8,128)(2,1)S(1)} %get-tuple-element.186), channel_id=1, source_target_pairs={{8,0},{16,8},{24,16},{32,24},{40,32},{48,40},{56,48},{64,56},{72,6... | collective-permute-start | bytes 6152 | tf_op jit(solution)/shard_map/ppermute | solution.py:22
  19.5 35.4 %collective-permute-start.4 = (bf16[8,1,8,128]{3,2,0,1:T(8,128)(2,1)S(1)}, bf16[8,1,8,128]{3,2,0,1:T(8,128)(2,1)S(1)}, u32[]{:S(2)}, u32[]{:S(2)}) collective-permute-start(bf16[8,1,8,128]{3,2,0,1:T(8,128)(2,1)S(1)} %get-tuple-element.159), channel_id=1, source_target_pairs={{0,8},{8,16},{16,24},{24,32},{32,40},{40,48},{48,56},{56,64},{64,7... | collective-permute-start | bytes 49160 | tf_op jit(solution)/shard_map/ppermute | solution.py:19
  21.4 33.4 %collective-permute-start.5 = (bf16[8,1,8,128]{3,2,0,1:T(8,128)(2,1)S(1)}, bf16[8,1,8,128]{3,2,0,1:T(8,128)(2,1)S(1)}, u32[]{:S(2)}, u32[]{:S(2)}) collective-permute-start(bf16[8,1,8,128]{3,2,0,1:T(8,128)(2,1)S(1)} %get-tuple-element.160), channel_id=1, source_target_pairs={{8,0},{16,8},{24,16},{32,24},{40,32},{48,40},{56,48},{64,56},{72,6... | collective-permute-start | bytes 49160 | tf_op jit(solution)/shard_map/ppermute | solution.py:22
  28.1 32.4 %collective-permute-start.20 = (bf16[8,1,8,128]{3,2,0,1:T(8,128)(2,1)S(1)}, bf16[8,1,8,128]{3,2,0,1:T(8,128)(2,1)S(1)}, u32[]{:S(2)}, u32[]{:S(2)}) collective-permute-start(bf16[8,1,8,128]{3,2,0,1:T(8,128)(2,1)S(1)} %get-tuple-element.167), channel_id=1, source_target_pairs={{0,8},{8,16},{16,24},{24,32},{32,40},{40,48},{48,56},{56,64},{64,7... | collective-permute-start | bytes 49160 | tf_op jit(solution)/shard_map/ppermute | solution.py:19
  45.6 8.9 %collective-permute-start.3 = (bf16[10,1,128]{2,1,0:T(2,128)(2,1)S(1)}, bf16[10,1,128]{2,1,0:T(2,128)(2,1)S(1)}, u32[]{:S(2)}, u32[]{:S(2)}) collective-permute-start(bf16[10,1,128]{2,1,0:T(2,128)(2,1)S(1)} %get-tuple-element.184), channel_id=1, source_target_pairs={{1,0},{2,1},{3,2},{4,3},{5,4},{6,5},{7,6},{9,8},{10,9},{11,10},{12... | collective-permute-start | bytes 7688 | tf_op jit(solution)/shard_map/ppermute | solution.py:22
  48.1 12.4 %collective-permute-start.21 = (bf16[8,1,8,128]{3,2,0,1:T(8,128)(2,1)S(1)}, bf16[8,1,8,128]{3,2,0,1:T(8,128)(2,1)S(1)}, u32[]{:S(2)}, u32[]{:S(2)}) collective-permute-start(bf16[8,1,8,128]{3,2,0,1:T(8,128)(2,1)S(1)} %get-tuple-element.168), channel_id=1, source_target_pairs={{8,0},{16,8},{24,16},{32,24},{40,32},{48,40},{56,48},{64,56},{72,6... | collective-permute-start | bytes 49160 | tf_op jit(solution)/shard_map/ppermute | solution.py:22
  54.9 11.5 %collective-permute-start.6 = (bf16[8,10,1,128]{3,2,0,1:T(2,128)(2,1)S(1)}, bf16[8,10,1,128]{3,2,0,1:T(2,128)(2,1)S(1)}, u32[]{:S(2)}, u32[]{:S(2)}) collective-permute-start(bf16[8,10,1,128]{3,2,0,1:T(2,128)(2,1)S(1)} %get-tuple-element.143), channel_id=1, source_target_pairs={{0,1},{1,2},{2,3},{3,4},{4,5},{5,6},{6,7},{8,9},{9,10},{10,11},{11... | collective-permute-start | bytes 61448 | tf_op jit(solution)/shard_map/ppermute | solution.py:19
  60.6 8.4 %collective-permute-start.22 = (bf16[8,10,1,128]{3,2,0,1:T(2,128)(2,1)S(1)}, bf16[8,10,1,128]{3,2,0,1:T(2,128)(2,1)S(1)}, u32[]{:S(2)}, u32[]{:S(2)}) collective-permute-start(bf16[8,10,1,128]{3,2,0,1:T(2,128)(2,1)S(1)} %get-tuple-element.151), channel_id=1, source_target_pairs={{0,1},{1,2},{2,3},{3,4},{4,5},{5,6},{6,7},{8,9},{9,10},{10,11},{11... | collective-permute-start | bytes 61448 | tf_op jit(solution)/shard_map/ppermute | solution.py:19
  72.6 17.5 %collective-permute-start.8 = (bf16[8,1,8,128]{3,2,0,1:T(8,128)(2,1)S(1)}, bf16[8,1,8,128]{3,2,0,1:T(8,128)(2,1)S(1)}, u32[]{:S(2)}, u32[]{:S(2)}) collective-permute-start(bf16[8,1,8,128]{3,2,0,1:T(8,128)(2,1)S(1)} %get-tuple-element.157), channel_id=1, source_target_pairs={{0,8},{8,16},{16,24},{24,32},{32,40},{40,48},{48,56},{56,64},{64,7... | collective-permute-start | bytes 49160 | tf_op jit(solution)/shard_map/ppermute | solution.py:19
  74.5 15.5 %collective-permute-start.9 = (bf16[8,1,8,128]{3,2,0,1:T(8,128)(2,1)S(1)}, bf16[8,1,8,128]{3,2,0,1:T(8,128)(2,1)S(1)}, u32[]{:S(2)}, u32[]{:S(2)}) collective-permute-start(bf16[8,1,8,128]{3,2,0,1:T(8,128)(2,1)S(1)} %get-tuple-element.158), channel_id=1, source_target_pairs={{8,0},{16,8},{24,16},{32,24},{40,32},{48,40},{56,48},{64,56},{72,6... | collective-permute-start | bytes 49160 | tf_op jit(solution)/shard_map/ppermute | solution.py:22
  81.3 13.6 %collective-permute-start.24 = (bf16[8,1,8,128]{3,2,0,1:T(8,128)(2,1)S(1)}, bf16[8,1,8,128]{3,2,0,1:T(8,128)(2,1)S(1)}, u32[]{:S(2)}, u32[]{:S(2)}) collective-permute-start(bf16[8,1,8,128]{3,2,0,1:T(8,128)(2,1)S(1)} %get-tuple-element.165), channel_id=1, source_target_pairs={{0,8},{8,16},{16,24},{24,32},{32,40},{40,48},{48,56},{56,64},{64,7... | collective-permute-start | bytes 49160 | tf_op jit(solution)/shard_map/ppermute | solution.py:19
  83.3 11.7 %collective-permute-start.25 = (bf16[8,1,8,128]{3,2,0,1:T(8,128)(2,1)S(1)}, bf16[8,1,8,128]{3,2,0,1:T(8,128)(2,1)S(1)}, u32[]{:S(2)}, u32[]{:S(2)}) collective-permute-start(bf16[8,1,8,128]{3,2,0,1:T(8,128)(2,1)S(1)} %get-tuple-element.166), channel_id=1, source_target_pairs={{8,0},{16,8},{24,16},{32,24},{40,32},{48,40},{56,48},{64,56},{72,6... | collective-permute-start | bytes 49160 | tf_op jit(solution)/shard_map/ppermute | solution.py:22
  90.1 12.9 %collective-permute-start.10 = (bf16[8,10,1,128]{3,2,0,1:T(2,128)(2,1)S(1)}, bf16[8,10,1,128]{3,2,0,1:T(2,128)(2,1)S(1)}, u32[]{:S(2)}, u32[]{:S(2)}) collective-permute-start(bf16[8,10,1,128]{3,2,0,1:T(2,128)(2,1)S(1)} %get-tuple-element.141), channel_id=1, source_target_pairs={{0,1},{1,2},{2,3},{3,4},{4,5},{5,6},{6,7},{8,9},{9,10},{10,11},{11... | collective-permute-start | bytes 61448 | tf_op jit(solution)/shard_map/ppermute | solution.py:19
  93.7 9.4 %collective-permute-start.11 = (bf16[8,10,1,128]{3,2,0,1:T(2,128)(2,1)S(1)}, bf16[8,10,1,128]{3,2,0,1:T(2,128)(2,1)S(1)}, u32[]{:S(2)}, u32[]{:S(2)}) collective-permute-start(bf16[8,10,1,128]{3,2,0,1:T(2,128)(2,1)S(1)} %get-tuple-element.142), channel_id=1, source_target_pairs={{1,0},{2,1},{3,2},{4,3},{5,4},{6,5},{7,6},{9,8},{10,9},{11,10},{12... | collective-permute-start | bytes 61448 | tf_op jit(solution)/shard_map/ppermute | solution.py:22
  95.1 9.6 %collective-permute-start.26 = (bf16[8,10,1,128]{3,2,0,1:T(2,128)(2,1)S(1)}, bf16[8,10,1,128]{3,2,0,1:T(2,128)(2,1)S(1)}, u32[]{:S(2)}, u32[]{:S(2)}) collective-permute-start(bf16[8,10,1,128]{3,2,0,1:T(2,128)(2,1)S(1)} %get-tuple-element.149), channel_id=1, source_target_pairs={{0,1},{1,2},{2,3},{3,4},{4,5},{5,6},{6,7},{8,9},{9,10},{10,11},{11... | collective-permute-start | bytes 61448 | tf_op jit(solution)/shard_map/ppermute | solution.py:19
  111.4 17.7 %collective-permute-start.12 = (bf16[8,1,8,128]{3,2,0,1:T(8,128)(2,1)S(1)}, bf16[8,1,8,128]{3,2,0,1:T(8,128)(2,1)S(1)}, u32[]{:S(2)}, u32[]{:S(2)}) collective-permute-start(bf16[8,1,8,128]{3,2,0,1:T(8,128)(2,1)S(1)} %get-tuple-element.155), channel_id=1, source_target_pairs={{0,8},{8,16},{16,24},{24,32},{32,40},{40,48},{48,56},{56,64},{64,7... | collective-permute-start | bytes 49160 | tf_op jit(solution)/shard_map/ppermute | solution.py:19
  113.5 15.5 %collective-permute-start.13 = (bf16[8,1,8,128]{3,2,0,1:T(8,128)(2,1)S(1)}, bf16[8,1,8,128]{3,2,0,1:T(8,128)(2,1)S(1)}, u32[]{:S(2)}, u32[]{:S(2)}) collective-permute-start(bf16[8,1,8,128]{3,2,0,1:T(8,128)(2,1)S(1)} %get-tuple-element.156), channel_id=1, source_target_pairs={{8,0},{16,8},{24,16},{32,24},{40,32},{48,40},{56,48},{64,56},{72,6... | collective-permute-start | bytes 49160 | tf_op jit(solution)/shard_map/ppermute | solution.py:22
  120.3 14.0 %collective-permute-start.28 = (bf16[8,1,8,128]{3,2,0,1:T(8,128)(2,1)S(1)}, bf16[8,1,8,128]{3,2,0,1:T(8,128)(2,1)S(1)}, u32[]{:S(2)}, u32[]{:S(2)}) collective-permute-start(bf16[8,1,8,128]{3,2,0,1:T(8,128)(2,1)S(1)} %get-tuple-element.163), channel_id=1, source_target_pairs={{0,8},{8,16},{16,24},{24,32},{32,40},{40,48},{48,56},{56,64},{64,7... | collective-permute-start | bytes 49160 | tf_op jit(solution)/shard_map/ppermute | solution.py:19
  122.3 12.1 %collective-permute-start.29 = (bf16[8,1,8,128]{3,2,0,1:T(8,128)(2,1)S(1)}, bf16[8,1,8,128]{3,2,0,1:T(8,128)(2,1)S(1)}, u32[]{:S(2)}, u32[]{:S(2)}) collective-permute-start(bf16[8,1,8,128]{3,2,0,1:T(8,128)(2,1)S(1)} %get-tuple-element.164), channel_id=1, source_target_pairs={{8,0},{16,8},{24,16},{32,24},{40,32},{48,40},{56,48},{64,56},{72,6... | collective-permute-start | bytes 49160 | tf_op jit(solution)/shard_map/ppermute | solution.py:22
  129.1 11.9 %collective-permute-start.14 = (bf16[8,10,1,128]{3,2,0,1:T(2,128)(2,1)S(1)}, bf16[8,10,1,128]{3,2,0,1:T(2,128)(2,1)S(1)}, u32[]{:S(2)}, u32[]{:S(2)}) collective-permute-start(bf16[8,10,1,128]{3,2,0,1:T(2,128)(2,1)S(1)} %get-tuple-element.139), channel_id=1, source_target_pairs={{0,1},{1,2},{2,3},{3,4},{4,5},{5,6},{6,7},{8,9},{9,10},{10,11},{11... | collective-permute-start | bytes 61448 | tf_op jit(solution)/shard_map/ppermute | solution.py:19
  149.5 17.3 %collective-permute-start.16 = (bf16[8,1,8,128]{3,2,0,1:T(8,128)(2,1)S(1)}, bf16[8,1,8,128]{3,2,0,1:T(8,128)(2,1)S(1)}, u32[]{:S(2)}, u32[]{:S(2)}) collective-permute-start(bf16[8,1,8,128]{3,2,0,1:T(8,128)(2,1)S(1)} %get-tuple-element.153), channel_id=1, source_target_pairs={{0,8},{8,16},{16,24},{24,32},{32,40},{40,48},{48,56},{56,64},{64,7... | collective-permute-start | bytes 49160 | tf_op jit(solution)/shard_map/ppermute | solution.py:19
  151.4 15.4 %collective-permute-start.17 = (bf16[8,1,8,128]{3,2,0,1:T(8,128)(2,1)S(1)}, bf16[8,1,8,128]{3,2,0,1:T(8,128)(2,1)S(1)}, u32[]{:S(2)}, u32[]{:S(2)}) collective-permute-start(bf16[8,1,8,128]{3,2,0,1:T(8,128)(2,1)S(1)} %get-tuple-element.154), channel_id=1, source_target_pairs={{8,0},{16,8},{24,16},{32,24},{40,32},{48,40},{56,48},{64,56},{72,6... | collective-permute-start | bytes 49160 | tf_op jit(solution)/shard_map/ppermute | solution.py:22
  158.2 13.9 %collective-permute-start.32 = (bf16[8,1,8,128]{3,2,0,1:T(8,128)(2,1)S(1)}, bf16[8,1,8,128]{3,2,0,1:T(8,128)(2,1)S(1)}, u32[]{:S(2)}, u32[]{:S(2)}) collective-permute-start(bf16[8,1,8,128]{3,2,0,1:T(8,128)(2,1)S(1)} %get-tuple-element.161), channel_id=1, source_target_pairs={{0,8},{8,16},{16,24},{24,32},{32,40},{40,48},{48,56},{56,64},{64,7... | collective-permute-start | bytes 49160 | tf_op jit(solution)/shard_map/ppermute | solution.py:19
  160.2 12.0 %collective-permute-start.33 = (bf16[8,1,8,128]{3,2,0,1:T(8,128)(2,1)S(1)}, bf16[8,1,8,128]{3,2,0,1:T(8,128)(2,1)S(1)}, u32[]{:S(2)}, u32[]{:S(2)}) collective-permute-start(bf16[8,1,8,128]{3,2,0,1:T(8,128)(2,1)S(1)} %get-tuple-element.162), channel_id=1, source_target_pairs={{8,0},{16,8},{24,16},{32,24},{40,32},{48,40},{56,48},{64,56},{72,6... | collective-permute-start | bytes 49160 | tf_op jit(solution)/shard_map/ppermute | solution.py:22
  166.9 11.3 %collective-permute-start.18 = (bf16[8,10,1,128]{3,2,0,1:T(2,128)(2,1)S(1)}, bf16[8,10,1,128]{3,2,0,1:T(2,128)(2,1)S(1)}, u32[]{:S(2)}, u32[]{:S(2)}) collective-permute-start(bf16[8,10,1,128]{3,2,0,1:T(2,128)(2,1)S(1)} %get-tuple-element.137), channel_id=1, source_target_pairs={{0,1},{1,2},{2,3},{3,4},{4,5},{5,6},{6,7},{8,9},{9,10},{10,11},{11... | collective-permute-start | bytes 61448 | tf_op jit(solution)/shard_map/ppermute | solution.py:19
  172.2 18.7 %collective-permute-start.34 = (bf16[8,10,1,128]{3,2,0,1:T(2,128)(2,1)S(1)}, bf16[8,10,1,128]{3,2,0,1:T(2,128)(2,1)S(1)}, u32[]{:S(2)}, u32[]{:S(2)}) collective-permute-start(bf16[8,10,1,128]{3,2,0,1:T(2,128)(2,1)S(1)} %get-tuple-element.145), channel_id=1, source_target_pairs={{0,1},{1,2},{2,3},{3,4},{4,5},{5,6},{6,7},{8,9},{9,10},{10,11},{11... | collective-permute-start | bytes 61448 | tf_op jit(solution)/shard_map/ppermute | solution.py:19
  176.9 14.0 %collective-permute-start.35 = (bf16[8,10,1,128]{3,2,0,1:T(2,128)(2,1)S(1)}, bf16[8,10,1,128]{3,2,0,1:T(2,128)(2,1)S(1)}, u32[]{:S(2)}, u32[]{:S(2)}) collective-permute-start(bf16[8,10,1,128]{3,2,0,1:T(2,128)(2,1)S(1)} %get-tuple-element.146), channel_id=1, source_target_pairs={{1,0},{2,1},{3,2},{4,3},{5,4},{6,5},{7,6},{9,8},{10,9},{11,10},{12... | collective-permute-start | bytes 61448 | tf_op jit(solution)/shard_map/ppermute | solution.py:22
  180.4 18.6 %all-to-all-start = ((bf16[32,8,8,128]{3,2,0,1:T(8,128)(2,1)}), bf16[32,8,8,128]{3,2,0,1:T(8,128)(2,1)S(1)}, u32[]{:S(2)}, u32[]{:S(2)}) async-start(bf16[32,8,8,128]{3,2,0,1:T(8,128)(2,1)} %pad_maximum_fusion.1), calls=%async_computation | async-start | bytes 1048576 | tf_op jit(solution)/shard_map/all_to_all | solution.py:165
  199.0 11.7 %all-to-all-start.1 = ((bf16[32,8,8,128]{3,2,0,1:T(8,128)(2,1)}), bf16[32,8,8,128]{3,2,0,1:T(8,128)(2,1)S(1)}, u32[]{:S(2)}, u32[]{:S(2)}) async-start(bf16[32,8,8,128]{3,2,0,1:T(8,128)(2,1)} %pad_maximum_fusion.2), calls=%async_computation.1 | async-start | bytes 1048576 | tf_op jit(solution)/shard_map/all_to_all | solution.py:165
  202.5 277.4 %all-reduce.24.cloned.1.call-start = ((), (), s32[]{:S(2)}) async-start(), calls=%async_computation.2 | async-start | bytes 983040 | tf_op jit(solution)/shard_map/psum | solution.py:183
  214.6 357.8 %all-reduce.26.cloned.1.call-start = ((), (), s32[]{:S(2)}) async-start(), calls=%async_computation.3 | async-start | bytes 983040 | tf_op jit(solution)/shard_map/psum | solution.py:183
  (18 other events, 466.0 us)
Sparse Core Ops, SparseCore 0:
  214.7 265.1 all-reduce.23
  482.6 89.7 all-reduce.25
